TPU v7x, 32 devices: a whole 2x2x4 slice. The times are simulated.
32 devices in a mesh: row: 8 (over z, y), col: 4 (over x, core).
Axes of the slice: x: 2, y: 2, z: 4, core: 2. Of those that a mesh axis runs over, the one named last changes fastest.
Arguments:
- examples: bfloat16 [8192, 1024], P('row'), may hold values from -40 to 40
- targets: float32 [8192, 64], P('row'), may hold values from -6 to 6
- landmark_rows: int32 [8192], P('col'), may hold values from 0 to 1023
- ainv: float32 [4, 8, 256, 8192], P(None, 'row', None, 'col'), as said below
- tinv_t: float32 [4, 8, 256, 8192], P(None, 'row', None, 'col'), as said below
Outputs:
- solution: float32 [8192, 64], P('col')
- weights: float32 [8192, 64], P('col')
Inputs may be any that keep to these rules, and one draw needn't show every extreme that they name: `landmark_rows`: landmark m is a row of example block ((m mod 2048) // 256); the value is its place within that block. `ainv`: the preconditioner's factor A inverse, in landmark order. `tinv_t`: the preconditioner's factor T inverse, transposed, in landmark order.
All inputs are finite; a program needn't handle non-finite values.
Results may differ from a plain program's by a relative error of at most 0.0003.
Values may be sent and summed in bfloat16 or wider, within the bound.
A program may use at most 128 MiB of HBM per device.

v0:
```python
import math
import jax
import jax.numpy as jnp
from jax import lax
from jax.sharding import PartitionSpec as P

D = 1024
ITERS = 2
LAMBDA = 0.001
EPSILON = 1e-06
HIGHEST = lax.Precision.HIGHEST


def kernel_tile(rows_data, landmarks, sq_lands):
    sq_rows = jnp.sum(jnp.square(rows_data.astype(jnp.float32)), axis=1)
    products = lax.dot_general(
        rows_data, landmarks, (((1,), (1,)), ((), ())), preferred_element_type=jnp.float32
    )
    return jnp.exp(-(sq_rows[:, None] + sq_lands[None, :] - 2.0 * products) / D)


def contract_rows(matrix, vectors):
    return lax.dot_general(
        matrix,
        vectors,
        (((0,), (0,)), ((), ())),
        precision=HIGHEST,
        preferred_element_type=jnp.float32,
    )


def times_matrix(matrix, vectors):
    return jnp.dot(matrix, vectors, precision=HIGHEST, preferred_element_type=jnp.float32)


def col_total(values):
    return lax.psum(values, "col")


def row_total(values):
    return lax.psum(values, "row")


def dot_total(values):
    return lax.psum(values, "col")


def column_sums(first, second):
    return jnp.sum(first * second, axis=0)


def shards(examples, targets, landmark_rows, ainv, tinv_t):
    row_count = lax.axis_size("row")
    total_rows = examples.shape[0] * row_count
    tile_width = landmark_rows.shape[0]
    owned_count = tile_width // row_count
    first_owned = lax.axis_index("row") * owned_count
    owned_ids = lax.dynamic_slice_in_dim(landmark_rows, first_owned, owned_count, 0)
    owned = jnp.take(examples, owned_ids, axis=0)
    landmarks = lax.all_gather(owned, "row", axis=0, tiled=True)
    sq_lands = jnp.sum(jnp.square(landmarks.astype(jnp.float32)), axis=1)
    kernel = kernel_tile(examples, landmarks, sq_lands)
    factor_a = ainv.reshape(-1, tile_width)
    factor_t = tinv_t.reshape(-1, tile_width)
    kernel_targets = row_total(contract_rows(kernel, targets))
    mixed = col_total(times_matrix(factor_t, kernel_targets))
    right_side = row_total(contract_rows(factor_a, mixed)) / math.sqrt(total_rows)
    solution = jnp.zeros(right_side.shape, jnp.float32)
    residual = right_side
    direction = right_side
    norm_now = dot_total(column_sums(residual, residual))
    for iteration in range(ITERS):
        mixed_in = col_total(times_matrix(factor_a, direction))
        lifted = row_total(contract_rows(factor_t, mixed_in))
        example_vals = lax.psum(times_matrix(kernel, lifted).astype(jnp.bfloat16), "col").astype(
            jnp.float32
        )
        local_back = contract_rows(kernel, example_vals)
        back = row_total(local_back)
        curvature = None
        lowered = col_total(times_matrix(factor_t, back))
        applied = row_total(contract_rows(factor_a, lowered / total_rows + LAMBDA * mixed_in))
        applied, curvature = (applied, curvature)
        step_size = norm_now / dot_total(column_sums(direction, applied))
        solution = solution + step_size * direction
        residual = residual - step_size * applied
        norm_next = dot_total(column_sums(residual, residual))
        direction = residual + norm_next / (norm_now + EPSILON) * direction
        norm_now = norm_next
    weights = row_total(contract_rows(factor_t, col_total(times_matrix(factor_a, solution))))
    return (solution, weights)


def solution(mesh):
    return jax.shard_map(
        shards,
        mesh=mesh,
        in_specs=(
            P("row", None),
            P("row", None),
            P("col"),
            P(None, "row", None, "col"),
            P(None, "row", None, "col"),
        ),
        out_specs=(P("col", None), P("col", None)),
        check_vma=False,
    )
```

profile of v0, /device:TPU:0, one launch (start us, length us, event | category | flops | bytes accessed | tf_op | source)
XLA Modules:
  0.0 1241.8 jit_solution(5362592691679920946)
XLA Ops:
  7.2 0.9 compare_and_fusion
  8.2 3.4 gather_fusion
  12.6 2.1 multiply_reduce_fusion.1
  14.7 74.1 %all-gather.2.cloned.1.call-done = bf16[2048,1024]{1,0:T(8,128)(2,1)} async-done(((bf16[256,1024]{1,0:T(8,128)(2,1)}), bf16[2048,1024]{1,0:T(8,128)(2,1)}) %all-gather.2.cloned.1.call-update) | async-done | bytes 4194320 | tf_op jit(solution)/shard_map/all_gather | solution.py:60
  88.8 3.1 multiply_reduce_fusion
  91.9 6.9 fusion.2
  98.8 3.2 copy-done.1
  102.0 7.7 fusion.21
  110.0 76.3 %all-reduce.19.cloned.1.call-done = f32[2048,64]{1,0:T(8,128)} async-done(((f32[2048,64]{1,0:T(8,128)}), f32[2048,64]{1,0:T(8,128)}) %all-reduce.19.cloned.1.call-update) | async-done | bytes 524304 | tf_op jit(solution)/shard_map/psum | solution.py:41
  186.3 12.7 %convolution_bitcast_fusion.11 = f32[1024,64]{0,1:T(8,128)} fusion(f32[2048,64]{1,0:T(8,128)} %all-reduce.19.cloned.1.call-done, f32[1024,2048]{1,0:T(8,128)} %bitcast.72), kind=kOutput, calls=%fused_computation.20 | convolution fusion | flops 1610612736 | bytes 9175040 | tf_op jit(solution)/shard_map/dot_general | solution.py:33
  199.1 31.7 %all-reduce.21.cloned.1.call-done = f32[1024,64]{0,1:T(8,128)} async-done(((f32[1024,64]{0,1:T(8,128)}), f32[1024,64]{0,1:T(8,128)}) %all-reduce.21.cloned.1.call-update) | async-done | bytes 262160 | tf_op jit(solution)/shard_map/psum | solution.py:37
  230.7 9.4 convolution_bitcast_fusion.5
  240.6 72.1 %all-reduce.23.cloned.1.call-done = f32[2048,64]{0,1:T(8,128)} async-done(((f32[2048,64]{0,1:T(8,128)}), f32[2048,64]{0,1:T(8,128)}) %all-reduce.23.cloned.1.call-update) | async-done | bytes 524304 | tf_op jit(solution)/shard_map/psum | solution.py:41
  312.7 12.3 convolution_bitcast_fusion.8
  325.1 31.3 %all-reduce.25.cloned.1.call-done = f32[1024,64]{0,1:T(8,128)} async-done(((f32[1024,64]{0,1:T(8,128)}), f32[1024,64]{0,1:T(8,128)}) %all-reduce.25.cloned.1.call-update) | async-done | bytes 262160 | tf_op jit(solution)/shard_map/psum | solution.py:37
  356.4 9.4 convolution_bitcast_fusion.4
  366.1 72.3 %all-reduce.27.cloned.1.call-done = f32[2048,64]{0,1:T(8,128)} async-done(((f32[2048,64]{0,1:T(8,128)}), f32[2048,64]{0,1:T(8,128)}) %all-reduce.27.cloned.1.call-update) | async-done | bytes 524304 | tf_op jit(solution)/shard_map/psum | solution.py:41
  438.4 16.3 %convolution_convert_fusion.1 = bf16[1024,64]{1,0:T(8,128)(2,1)} fusion(f32[1024,2048]{0,1:T(8,128)} %copy-done.1, f32[2048,64]{0,1:T(8,128)} %all-reduce.27.cloned.1.call-done), kind=kOutput, calls=%fused_computation.14 | convolution fusion | flops 1610678272 | bytes 9043968 | tf_op jit(solution)/shard_map/dot_general | solution.py:33
  454.8 31.4 %all-reduce.29.cloned.1.call-done = bf16[1024,64]{1,0:T(8,128)(2,1)} async-done(((bf16[1024,64]{1,0:T(8,128)(2,1)}), bf16[1024,64]{1,0:T(8,128)(2,1)}) %all-reduce.29.cloned.1.call-update) | async-done | bytes 131088 | tf_op jit(solution)/shard_map/psum | solution.py:75
  486.1 8.2 fusion.22
  494.7 78.0 %all-reduce.31.cloned.1.call-done = f32[2048,64]{1,0:T(8,128)} async-done(((f32[2048,64]{1,0:T(8,128)}), f32[2048,64]{1,0:T(8,128)}) %all-reduce.31.cloned.1.call-update) | async-done | bytes 524304 | tf_op jit(solution)/shard_map/psum | solution.py:41
  572.7 12.7 %convolution_bitcast_fusion.10 = f32[1024,64]{0,1:T(8,128)} fusion(f32[2048,64]{1,0:T(8,128)} %all-reduce.31.cloned.1.call-done, f32[1024,2048]{1,0:T(8,128)} %bitcast.74), kind=kOutput, calls=%fused_computation.19 | convolution fusion | flops 1610612736 | bytes 9175040 | tf_op jit(solution)/shard_map/dot_general | solution.py:33
  585.5 31.6 %all-reduce.33.cloned.1.call-done = f32[1024,64]{0,1:T(8,128)} async-done(((f32[1024,64]{0,1:T(8,128)}), f32[1024,64]{0,1:T(8,128)}) %all-reduce.33.cloned.1.call-update) | async-done | bytes 262160 | tf_op jit(solution)/shard_map/psum | solution.py:37
  617.2 9.4 convolution_bitcast_fusion.3
  626.6 72.5 %all-reduce.35.cloned.1.call-done = f32[2048,64]{0,1:T(8,128)} async-done(((f32[2048,64]{0,1:T(8,128)}), f32[2048,64]{0,1:T(8,128)}) %all-reduce.35.cloned.1.call-update) | async-done | bytes 524304 | tf_op jit(solution)/shard_map/psum | solution.py:41
  699.1 1.2 multiply_reduce_fusion.4
  700.3 5.7 all-reduce
  706.0 1.3 multiply_reduce_fusion.3
  707.3 7.0 psum.158
  714.3 12.4 convolution_bitcast_fusion.7
  726.8 30.8 %all-reduce.37.cloned.1.call-done = f32[1024,64]{0,1:T(8,128)} async-done(((f32[1024,64]{0,1:T(8,128)}), f32[1024,64]{0,1:T(8,128)}) %all-reduce.37.cloned.1.call-update) | async-done | bytes 262160 | tf_op jit(solution)/shard_map/psum | solution.py:37
  757.6 9.4 convolution_bitcast_fusion.2
  767.2 72.2 %all-reduce.39.cloned.1.call-done = f32[2048,64]{0,1:T(8,128)} async-done(((f32[2048,64]{0,1:T(8,128)}), f32[2048,64]{0,1:T(8,128)}) %all-reduce.39.cloned.1.call-update) | async-done | bytes 524304 | tf_op jit(solution)/shard_map/psum | solution.py:41
  839.5 16.3 %convolution_convert_fusion = bf16[1024,64]{1,0:T(8,128)(2,1)} fusion(f32[1024,2048]{0,1:T(8,128)} %copy-done.1, f32[2048,64]{0,1:T(8,128)} %all-reduce.39.cloned.1.call-done), kind=kOutput, calls=%fused_computation.13 | convolution fusion | flops 1610678272 | bytes 9043968 | tf_op jit(solution)/shard_map/dot_general | solution.py:33
  855.9 31.4 %all-reduce.41.cloned.1.call-done = bf16[1024,64]{1,0:T(8,128)(2,1)} async-done(((bf16[1024,64]{1,0:T(8,128)(2,1)}), bf16[1024,64]{1,0:T(8,128)(2,1)}) %all-reduce.41.cloned.1.call-update) | async-done | bytes 131088 | tf_op jit(solution)/shard_map/psum | solution.py:75
  887.2 8.2 fusion.23
  895.8 78.0 %all-reduce.43.cloned.1.call-done = f32[2048,64]{1,0:T(8,128)} async-done(((f32[2048,64]{1,0:T(8,128)}), f32[2048,64]{1,0:T(8,128)}) %all-reduce.43.cloned.1.call-update) | async-done | bytes 524304 | tf_op jit(solution)/shard_map/psum | solution.py:41
  973.8 12.7 %convolution_bitcast_fusion.9 = f32[1024,64]{0,1:T(8,128)} fusion(f32[2048,64]{1,0:T(8,128)} %all-reduce.43.cloned.1.call-done, f32[1024,2048]{1,0:T(8,128)} %bitcast.76), kind=kOutput, calls=%fused_computation.18 | convolution fusion | flops 1610612736 | bytes 9175040 | tf_op jit(solution)/shard_map/dot_general | solution.py:33
  986.6 31.7 %all-reduce.45.cloned.1.call-done = f32[1024,64]{0,1:T(8,128)} async-done(((f32[1024,64]{0,1:T(8,128)}), f32[1024,64]{0,1:T(8,128)}) %all-reduce.45.cloned.1.call-update) | async-done | bytes 262160 | tf_op jit(solution)/shard_map/psum | solution.py:37
  1018.2 9.4 convolution_bitcast_fusion.1
  1027.7 72.5 %all-reduce.47.cloned.1.call-done = f32[2048,64]{0,1:T(8,128)} async-done(((f32[2048,64]{0,1:T(8,128)}), f32[2048,64]{0,1:T(8,128)}) %all-reduce.47.cloned.1.call-update) | async-done | bytes 524304 | tf_op jit(solution)/shard_map/psum | solution.py:41
  1100.2 1.3 multiply_reduce_fusion.2
  1101.6 5.9 psum.165
  1107.8 11.3 convolution_bitcast_fusion.6
  1119.1 31.5 %all-reduce.49.cloned.1.call-done = f32[1024,64]{0,1:T(8,128)} async-done(((f32[1024,64]{0,1:T(8,128)}), f32[1024,64]{0,1:T(8,128)}) %all-reduce.49.cloned.1.call-update) | async-done | bytes 262160 | tf_op jit(solution)/shard_map/psum | solution.py:37
  1150.7 9.4 convolution_bitcast_fusion
  1160.1 72.6 %all-reduce.51.cloned.1.call-done = f32[2048,64]{0,1:T(8,128)} async-done(((f32[2048,64]{0,1:T(8,128)}), f32[2048,64]{0,1:T(8,128)}) %all-reduce.51.cloned.1.call-update) | async-done | bytes 524304 | tf_op jit(solution)/shard_map/psum | solution.py:41
  1232.7 1.9 copy.24
  (57 shorter events, 3.7 us)
Async XLA Ops:
  7.2 94.8 %copy-start = (f32[1024,64]{0,1:T(8,128)S(1)}, f32[1024,64]{0,1:T(8,128)}, u32[]{:S(2)}) copy-start(f32[1024,64]{0,1:T(8,128)} %param.6) | copy-start | bytes 786436
  7.2 84.7 %copy-start.3 = (bf16[1024,1024]{1,0:T(8,128)(2,1)S(1)}, bf16[1024,1024]{1,0:T(8,128)(2,1)}, u32[]{:S(2)}) copy-start(bf16[1024,1024]{1,0:T(8,128)(2,1)} %param.5) | copy-start | bytes 6291460
  7.2 81.6 %all-gather.2.cloned.1.call-start = ((), (), s32[]{:S(2)}) async-start(), calls=%async_computation | async-start | bytes 4718592 | tf_op jit(solution)/shard_map/all_gather | solution.py:60
  12.5 173.8 %all-reduce.19.cloned.1.call-start = ((), (), s32[]{:S(2)}) async-start(), calls=%async_computation.1 | async-start | bytes 2097152 | tf_op jit(solution)/shard_map/psum | solution.py:41
  98.7 3.2 copy-start.1
  109.7 121.0 %all-reduce.21.cloned.1.call-start = ((), (), s32[]{:S(2)}) async-start(), calls=%async_computation.2 | async-start | bytes 524288 | tf_op jit(solution)/shard_map/psum | solution.py:37
  199.0 113.7 %all-reduce.23.cloned.1.call-start = ((), (), s32[]{:S(2)}) async-start(), calls=%async_computation.3 | async-start | bytes 1048576 | tf_op jit(solution)/shard_map/psum | solution.py:41
  240.2 116.2 %all-reduce.25.cloned.1.call-start = ((), (), s32[]{:S(2)}) async-start(), calls=%async_computation.4 | async-start | bytes 524288 | tf_op jit(solution)/shard_map/psum | solution.py:37
  325.0 113.4 %all-reduce.27.cloned.1.call-start = ((), (), s32[]{:S(2)}) async-start(), calls=%async_computation.5 | async-start | bytes 1048576 | tf_op jit(solution)/shard_map/psum | solution.py:41
  365.8 120.3 %all-reduce.29.cloned.1.call-start = ((), (), s32[]{:S(2)}) async-start(), calls=%async_computation.6 | async-start | bytes 524288 | tf_op jit(solution)/shard_map/psum | solution.py:75
  454.7 162.4 %copy-start.7 = (f32[1024,64]{0,1:T(8,128)S(1)}, f32[1024,64]{0,1:T(8,128)}, u32[]{:S(2)}) copy-start(f32[1024,64]{0,1:T(8,128)} %all-reduce.25.cloned.1.call-done) | copy-start | bytes 786436
  454.7 118.0 %all-reduce.31.cloned.1.call-start = ((), (), s32[]{:S(2)}) async-start(), calls=%async_computation.7 | async-start | bytes 2097152 | tf_op jit(solution)/shard_map/psum | solution.py:41
  494.4 204.7 %copy-start.2 = (f32[2048,64]{0,1:T(8,128)S(1)}, f32[2048,64]{0,1:T(8,128)}, u32[]{:S(2)}) copy-start(f32[2048,64]{0,1:T(8,128)} %all-reduce.23.cloned.1.call-done) | copy-start | bytes 1572868
  494.4 122.8 %all-reduce.33.cloned.1.call-start = ((), (), s32[]{:S(2)}) async-start(), calls=%async_computation.8 | async-start | bytes 524288 | tf_op jit(solution)/shard_map/psum | solution.py:37
  585.5 113.6 %all-reduce.35.cloned.1.call-start = ((), (), s32[]{:S(2)}) async-start(), calls=%async_computation.9 | async-start | bytes 1048576 | tf_op jit(solution)/shard_map/psum | solution.py:41
  626.6 131.0 %all-reduce.37.cloned.1.call-start = ((), (), s32[]{:S(2)}) async-start(), calls=%async_computation.10 | async-start | bytes 524288 | tf_op jit(solution)/shard_map/psum | solution.py:37
  726.8 112.7 %all-reduce.39.cloned.1.call-start = ((), (), s32[]{:S(2)}) async-start(), calls=%async_computation.11 | async-start | bytes 1048576 | tf_op jit(solution)/shard_map/psum | solution.py:41
  767.0 120.2 %all-reduce.41.cloned.1.call-start = ((), (), s32[]{:S(2)}) async-start(), calls=%async_computation.12 | async-start | bytes 524288 | tf_op jit(solution)/shard_map/psum | solution.py:75
  855.8 162.4 %copy-start.6 = (f32[1024,64]{0,1:T(8,128)S(1)}, f32[1024,64]{0,1:T(8,128)}, u32[]{:S(2)}) copy-start(f32[1024,64]{0,1:T(8,128)} %all-reduce.37.cloned.1.call-done) | copy-start | bytes 786436
  855.8 118.0 %all-reduce.43.cloned.1.call-start = ((), (), s32[]{:S(2)}) async-start(), calls=%async_computation.13 | async-start | bytes 2097152 | tf_op jit(solution)/shard_map/psum | solution.py:41
  895.5 204.7 %copy-start.4 = (f32[2048,64]{0,1:T(8,128)S(1)}, f32[2048,64]{0,1:T(8,128)}, u32[]{:S(2)}) copy-start(f32[2048,64]{0,1:T(8,128)} %all-reduce.35.cloned.1.call-done) | copy-start | bytes 1572868
  895.5 122.7 %all-reduce.45.cloned.1.call-start = ((), (), s32[]{:S(2)}) async-start(), calls=%async_computation.14 | async-start | bytes 524288 | tf_op jit(solution)/shard_map/psum | solution.py:37
  986.5 113.7 %all-reduce.47.cloned.1.call-start = ((), (), s32[]{:S(2)}) async-start(), calls=%async_computation.15 | async-start | bytes 1048576 | tf_op jit(solution)/shard_map/psum | solution.py:41
  1027.7 123.0 %all-reduce.49.cloned.1.call-start = ((), (), s32[]{:S(2)}) async-start(), calls=%async_computation.16 | async-start | bytes 524288 | tf_op jit(solution)/shard_map/psum | solution.py:37
  1107.8 52.3 %copy-start.5 = (f32[2048,64]{0,1:T(8,128)}, f32[2048,64]{0,1:T(8,128)S(1)}, u32[]{:S(2)}) copy-start(f32[2048,64]{0,1:T(8,128)S(1)} %multiply_add_fusion) | copy-start | bytes 1572868
  1119.1 113.6 %all-reduce.51.cloned.1.call-start = ((), (), s32[]{:S(2)}) async-start(), calls=%async_computation.17 | async-start | bytes 1048576 | tf_op jit(solution)/shard_map/psum | solution.py:41
Sparse Core Ops, SparseCore 0:
  12.7 76.0 all-gather.1
  109.9 76.3 all-reduce.18
  199.2 31.5 all-reduce.20
  240.3 72.3 all-reduce.22
  325.1 31.2 all-reduce.24
  366.0 72.3 all-reduce.26
  454.8 31.2 all-reduce.28
  494.5 78.1 all-reduce.30
  585.6 31.5 all-reduce.32
  626.7 72.3 all-reduce.34
  726.9 30.6 all-reduce.36
  767.1 72.3 all-reduce.38
  855.9 31.2 all-reduce.40
  895.6 78.1 all-reduce.42
  986.6 31.5 all-reduce.44
  1027.8 72.3 all-reduce.46
  1119.2 31.4 all-reduce.48
  1160.2 72.3 all-reduce.50
where the time goes:
time: 1250 us; the launch traced here: 1240 us
  waiting for transfers between devices  992 us (79%)
  matrix products  194 us (16%)
  blocking collectives  18.6 us (1%)
  between operations  14.9 us (1%)
    psum x9, waiting for transfers between devices, row_total(): return lax.psum(values, 'row')  667 us
    psum x6, waiting for transfers between devices, col_total(): return lax.psum(values, 'col')  189 us
    dot_general x8, matrix products, times_matrix(): jnp.dot(matrix, vectors, precision=HIGHEST, preferred_element_type=jnp.fl...  107 us
    dot_general x9, matrix products, contract_rows(): lax.dot_general(matrix, vectors, (((0,), (0,)), ((), ())), precision=HIGH...  80.7 us
    all_gather x1, waiting for transfers between devices, shards(): landmarks = lax.all_gather(owned, 'row', axis=0, tiled=True)  74.1 us
    psum x2, waiting for transfers between devices, shards(): lax.psum(times_matrix(kernel, lifted).astype(jnp.bfloat16), 'col')  62.7 us
  transfers between devices with their start and end apart: 18, of which 18 were waited for; matrix products, arithmetic and copies ran while one was open for 0% of the time, Pallas kernels for 0%

commit v1 on v0

--- a/solution.py
+++ b/solution.py
@@ -9,6 +9,11 @@
 LAMBDA = 0.001
 EPSILON = 1e-06
 HIGHEST = lax.Precision.HIGHEST
+
+
+def add_all(x, axis):
+    parts = lax.all_gather(x, axis)
+    return jnp.sum(parts, axis=0)
 
 
 def kernel_tile(rows_data, landmarks, sq_lands):
@@ -72,7 +77,7 @@
     for iteration in range(ITERS):
         mixed_in = col_total(times_matrix(factor_a, direction))
         lifted = row_total(contract_rows(factor_t, mixed_in))
-        example_vals = lax.psum(times_matrix(kernel, lifted).astype(jnp.bfloat16), "col").astype(
+        example_vals = add_all(times_matrix(kernel, lifted).astype(jnp.bfloat16), "col").astype(
             jnp.float32
         )
         local_back = contract_rows(kernel, example_vals)

time: 1250 us -> 1180 us (0.944)
  waiting for transfers between devices: 992 us -> 927 us
  matrix products: 194 us -> 177 us
  blocking collectives: 18.6 us -> 32.9 us
    psum x2 -> x0, waiting for transfers between devices: 62.7 us -> none  [shards(): lax.psum(times_matrix(kernel, lifted).astype(jnp.bfloat16), 'col')]
    dot_general x8, matrix products: 107 us -> 91.7 us  [times_matrix(): jnp.dot(matrix, vectors, precision=HIGHEST, preferred_element_type=jnp.fl...]
    all_gather x0 -> x2, blocking collectives: none -> 14.3 us  [add_all(): parts = lax.all_gather(x, axis)]
  transfers between devices with their start and end apart: 18 -> 16, of which waited for: 18 -> 16; matrix products, arithmetic and copies ran while one was open for 0% -> 0% of each run, Pallas kernels for 0% -> 0%
where the time goes in v1:
time: 1180 us
  waiting for transfers between devices  927 us (79%)
  matrix products  177 us (15%)
  blocking collectives  32.9 us (3%)
  between operations  14.6 us (1%)
  other arithmetic  12.5 us (1%)
    psum x9, waiting for transfers between devices, row_total(): return lax.psum(values, 'row')  664 us
    psum x6, waiting for transfers between devices, col_total(): return lax.psum(values, 'col')  189 us
    dot_general x8, matrix products, times_matrix(): jnp.dot(matrix, vectors, precision=HIGHEST, preferred_element_type=jnp.fl...  91.7 us
    dot_general x9, matrix products, contract_rows(): lax.dot_general(matrix, vectors, (((0,), (0,)), ((), ())), precision=HIGH...  78.8 us
    all_gather x1, waiting for transfers between devices, shards(): landmarks = lax.all_gather(owned, 'row', axis=0, tiled=True)  74.1 us
  transfers between devices with their start and end apart: 16, of which 16 were waited for; matrix products, arithmetic and copies ran while one was open for 0% of the time, Pallas kernels for 0%

profile of v1, /device:TPU:0, one launch (start us, length us, event | category | flops | bytes accessed | tf_op | source)
XLA Modules:
  0.0 1175.3 jit_solution(16420200129040761458)
XLA Ops:
  7.2 0.9 compare_and_fusion
  8.2 3.4 gather_fusion
  12.6 2.1 multiply_reduce_fusion.1
  14.7 74.1 %all-gather.4.cloned.1.call-done = bf16[2048,1024]{1,0:T(8,128)(2,1)} async-done(((bf16[256,1024]{1,0:T(8,128)(2,1)}), bf16[2048,1024]{1,0:T(8,128)(2,1)}) %all-gather.4.cloned.1.call-update) | async-done | bytes 4194320 | tf_op jit(solution)/shard_map/all_gather | solution.py:65
  88.8 3.1 multiply_reduce_fusion
  91.9 6.9 fusion.2
  98.8 3.2 copy-done.1
  102.0 7.7 fusion.21
  110.0 76.3 %all-reduce.17.cloned.1.call-done = f32[2048,64]{1,0:T(8,128)} async-done(((f32[2048,64]{1,0:T(8,128)}), f32[2048,64]{1,0:T(8,128)}) %all-reduce.17.cloned.1.call-update) | async-done | bytes 524304 | tf_op jit(solution)/shard_map/psum | solution.py:46
  186.3 12.7 %convolution_bitcast_fusion.11 = f32[1024,64]{0,1:T(8,128)} fusion(f32[2048,64]{1,0:T(8,128)} %all-reduce.17.cloned.1.call-done, f32[1024,2048]{1,0:T(8,128)} %bitcast.76), kind=kOutput, calls=%fused_computation.18 | convolution fusion | flops 1610612736 | bytes 9175040 | tf_op jit(solution)/shard_map/dot_general | solution.py:38
  199.1 31.7 %all-reduce.19.cloned.1.call-done = f32[1024,64]{0,1:T(8,128)} async-done(((f32[1024,64]{0,1:T(8,128)}), f32[1024,64]{0,1:T(8,128)}) %all-reduce.19.cloned.1.call-update) | async-done | bytes 262160 | tf_op jit(solution)/shard_map/psum | solution.py:42
  230.7 9.4 convolution_bitcast_fusion.5
  240.6 72.1 %all-reduce.21.cloned.1.call-done = f32[2048,64]{0,1:T(8,128)} async-done(((f32[2048,64]{0,1:T(8,128)}), f32[2048,64]{0,1:T(8,128)}) %all-reduce.21.cloned.1.call-update) | async-done | bytes 524304 | tf_op jit(solution)/shard_map/psum | solution.py:46
  312.7 12.3 %convolution_bitcast_fusion.8 = f32[1024,64]{0,1:T(8,128)} fusion(f32[1024,2048]{1,0:T(8,128)} %bitcast.71, f32[2048,64]{0,1:T(8,128)} %all-reduce.21.cloned.1.call-done), kind=kOutput, calls=%fused_computation.15 | convolution fusion | flops 1610743808 | bytes 9175040 | tf_op jit(solution)/shard_map/dot_general | solution.py:38
  325.1 31.3 %all-reduce.23.cloned.1.call-done = f32[1024,64]{0,1:T(8,128)} async-done(((f32[1024,64]{0,1:T(8,128)}), f32[1024,64]{0,1:T(8,128)}) %all-reduce.23.cloned.1.call-update) | async-done | bytes 262160 | tf_op jit(solution)/shard_map/psum | solution.py:42
  356.4 9.4 convolution_bitcast_fusion.4
  366.1 72.3 %all-reduce.25.cloned.1.call-done = f32[2048,64]{0,1:T(8,128)} async-done(((f32[2048,64]{0,1:T(8,128)}), f32[2048,64]{0,1:T(8,128)}) %all-reduce.25.cloned.1.call-update) | async-done | bytes 524304 | tf_op jit(solution)/shard_map/psum | solution.py:46
  438.4 8.8 convolution_convert_fusion.1
  447.2 7.1 all-gather
  455.4 7.3 fusion.22
  462.9 76.5 %all-reduce.27.cloned.1.call-done = f32[2048,64]{1,0:T(8,128)} async-done(((f32[2048,64]{1,0:T(8,128)}), f32[2048,64]{1,0:T(8,128)}) %all-reduce.27.cloned.1.call-update) | async-done | bytes 524304 | tf_op jit(solution)/shard_map/psum | solution.py:46
  539.5 12.7 %convolution_bitcast_fusion.10 = f32[1024,64]{0,1:T(8,128)} fusion(f32[2048,64]{1,0:T(8,128)} %all-reduce.27.cloned.1.call-done, f32[1024,2048]{1,0:T(8,128)} %bitcast.78), kind=kOutput, calls=%fused_computation.17 | convolution fusion | flops 1610612736 | bytes 9175040 | tf_op jit(solution)/shard_map/dot_general | solution.py:38
  552.3 31.7 %all-reduce.29.cloned.1.call-done = f32[1024,64]{0,1:T(8,128)} async-done(((f32[1024,64]{0,1:T(8,128)}), f32[1024,64]{0,1:T(8,128)}) %all-reduce.29.cloned.1.call-update) | async-done | bytes 262160 | tf_op jit(solution)/shard_map/psum | solution.py:42
  583.9 9.4 convolution_bitcast_fusion.3
  593.4 72.4 %all-reduce.31.cloned.1.call-done = f32[2048,64]{0,1:T(8,128)} async-done(((f32[2048,64]{0,1:T(8,128)}), f32[2048,64]{0,1:T(8,128)}) %all-reduce.31.cloned.1.call-update) | async-done | bytes 524304 | tf_op jit(solution)/shard_map/psum | solution.py:46
  665.8 1.2 multiply_reduce_fusion.4
  667.1 5.7 all-reduce
  672.7 1.3 multiply_reduce_fusion.3
  674.0 7.0 psum.143
  681.1 12.4 %convolution_bitcast_fusion.7 = f32[1024,64]{0,1:T(8,128)} fusion(f32[1024,2048]{1,0:T(8,128)} %bitcast.73, f32[2048,64]{0,1:T(8,128)S(1)} %copy-done.2, f32[2048,64]{0,1:T(8,128)} %all-reduce.31.cloned.1.call-done, f32[64]{0:T(128)S(1)} %fusion.15, f32[64]{0:T(128)S(1)} %get-tuple-element.7), kind=kOutput, calls=%fused_computation.14 | convolution fusion | flops 1611268096 | bytes 9699840 | tf_op jit(solution)/shard_map/dot_general | solution.py:38
  693.5 30.8 %all-reduce.33.cloned.1.call-done = f32[1024,64]{0,1:T(8,128)} async-done(((f32[1024,64]{0,1:T(8,128)}), f32[1024,64]{0,1:T(8,128)}) %all-reduce.33.cloned.1.call-update) | async-done | bytes 262160 | tf_op jit(solution)/shard_map/psum | solution.py:42
  724.3 9.4 convolution_bitcast_fusion.2
  734.0 72.2 %all-reduce.35.cloned.1.call-done = f32[2048,64]{0,1:T(8,128)} async-done(((f32[2048,64]{0,1:T(8,128)}), f32[2048,64]{0,1:T(8,128)}) %all-reduce.35.cloned.1.call-update) | async-done | bytes 524304 | tf_op jit(solution)/shard_map/psum | solution.py:46
  806.2 8.8 convolution_convert_fusion
  815.0 7.1 all-gather.1
  823.2 7.3 fusion.23
  830.9 76.8 %all-reduce.37.cloned.1.call-done = f32[2048,64]{1,0:T(8,128)} async-done(((f32[2048,64]{1,0:T(8,128)}), f32[2048,64]{1,0:T(8,128)}) %all-reduce.37.cloned.1.call-update) | async-done | bytes 524304 | tf_op jit(solution)/shard_map/psum | solution.py:46
  907.6 12.7 %convolution_bitcast_fusion.9 = f32[1024,64]{0,1:T(8,128)} fusion(f32[2048,64]{1,0:T(8,128)} %all-reduce.37.cloned.1.call-done, f32[1024,2048]{1,0:T(8,128)} %bitcast.80), kind=kOutput, calls=%fused_computation.16 | convolution fusion | flops 1610612736 | bytes 9175040 | tf_op jit(solution)/shard_map/dot_general | solution.py:38
  920.4 31.6 %all-reduce.39.cloned.1.call-done = f32[1024,64]{0,1:T(8,128)} async-done(((f32[1024,64]{0,1:T(8,128)}), f32[1024,64]{0,1:T(8,128)}) %all-reduce.39.cloned.1.call-update) | async-done | bytes 262160 | tf_op jit(solution)/shard_map/psum | solution.py:42
  952.1 9.4 convolution_bitcast_fusion.1
  961.6 72.4 %all-reduce.41.cloned.1.call-done = f32[2048,64]{0,1:T(8,128)} async-done(((f32[2048,64]{0,1:T(8,128)}), f32[2048,64]{0,1:T(8,128)}) %all-reduce.41.cloned.1.call-update) | async-done | bytes 524304 | tf_op jit(solution)/shard_map/psum | solution.py:46
  1034.0 1.3 multiply_reduce_fusion.2
  1035.3 5.9 psum.149
  1041.6 11.3 convolution_bitcast_fusion.6
  1052.9 31.6 %all-reduce.43.cloned.1.call-done = f32[1024,64]{0,1:T(8,128)} async-done(((f32[1024,64]{0,1:T(8,128)}), f32[1024,64]{0,1:T(8,128)}) %all-reduce.43.cloned.1.call-update) | async-done | bytes 262160 | tf_op jit(solution)/shard_map/psum | solution.py:42
  1084.5 9.4 convolution_bitcast_fusion
  1093.9 72.5 %all-reduce.45.cloned.1.call-done = f32[2048,64]{0,1:T(8,128)} async-done(((f32[2048,64]{0,1:T(8,128)}), f32[2048,64]{0,1:T(8,128)}) %all-reduce.45.cloned.1.call-update) | async-done | bytes 524304 | tf_op jit(solution)/shard_map/psum | solution.py:46
  1166.4 1.9 copy.22
  (57 shorter events, 5.7 us)
Async XLA Ops:
  7.2 94.8 %copy-start = (f32[1024,64]{0,1:T(8,128)S(1)}, f32[1024,64]{0,1:T(8,128)}, u32[]{:S(2)}) copy-start(f32[1024,64]{0,1:T(8,128)} %param.6) | copy-start | bytes 786436
  7.2 84.7 %copy-start.3 = (bf16[1024,1024]{1,0:T(8,128)(2,1)S(1)}, bf16[1024,1024]{1,0:T(8,128)(2,1)}, u32[]{:S(2)}) copy-start(bf16[1024,1024]{1,0:T(8,128)(2,1)} %param.5) | copy-start | bytes 6291460
  7.2 81.6 %all-gather.4.cloned.1.call-start = ((), (), s32[]{:S(2)}) async-start(), calls=%async_computation | async-start | bytes 4718592 | tf_op jit(solution)/shard_map/all_gather | solution.py:65
  12.5 173.8 %all-reduce.17.cloned.1.call-start = ((), (), s32[]{:S(2)}) async-start(), calls=%async_computation.1 | async-start | bytes 2097152 | tf_op jit(solution)/shard_map/psum | solution.py:46
  98.7 3.2 copy-start.1
  109.7 121.0 %all-reduce.19.cloned.1.call-start = ((), (), s32[]{:S(2)}) async-start(), calls=%async_computation.2 | async-start | bytes 524288 | tf_op jit(solution)/shard_map/psum | solution.py:42
  199.0 113.7 %all-reduce.21.cloned.1.call-start = ((), (), s32[]{:S(2)}) async-start(), calls=%async_computation.3 | async-start | bytes 1048576 | tf_op jit(solution)/shard_map/psum | solution.py:46
  240.2 116.2 %all-reduce.23.cloned.1.call-start = ((), (), s32[]{:S(2)}) async-start(), calls=%async_computation.4 | async-start | bytes 524288 | tf_op jit(solution)/shard_map/psum | solution.py:42
  325.0 113.4 %all-reduce.25.cloned.1.call-start = ((), (), s32[]{:S(2)}) async-start(), calls=%async_computation.5 | async-start | bytes 1048576 | tf_op jit(solution)/shard_map/psum | solution.py:46
  365.8 173.6 %all-reduce.27.cloned.1.call-start = ((), (), s32[]{:S(2)}) async-start(), calls=%async_computation.6 | async-start | bytes 2097152 | tf_op jit(solution)/shard_map/psum | solution.py:46
  455.4 128.6 %copy-start.7 = (f32[1024,64]{0,1:T(8,128)S(1)}, f32[1024,64]{0,1:T(8,128)}, u32[]{:S(2)}) copy-start(f32[1024,64]{0,1:T(8,128)} %all-reduce.23.cloned.1.call-done) | copy-start | bytes 786436
  462.7 203.2 %copy-start.2 = (f32[2048,64]{0,1:T(8,128)S(1)}, f32[2048,64]{0,1:T(8,128)}, u32[]{:S(2)}) copy-start(f32[2048,64]{0,1:T(8,128)} %all-reduce.21.cloned.1.call-done) | copy-start | bytes 1572868
  462.7 121.3 %all-reduce.29.cloned.1.call-start = ((), (), s32[]{:S(2)}) async-start(), calls=%async_computation.7 | async-start | bytes 524288 | tf_op jit(solution)/shard_map/psum | solution.py:42
  552.2 113.6 %all-reduce.31.cloned.1.call-start = ((), (), s32[]{:S(2)}) async-start(), calls=%async_computation.8 | async-start | bytes 1048576 | tf_op jit(solution)/shard_map/psum | solution.py:46
  593.4 131.0 %all-reduce.33.cloned.1.call-start = ((), (), s32[]{:S(2)}) async-start(), calls=%async_computation.9 | async-start | bytes 524288 | tf_op jit(solution)/shard_map/psum | solution.py:42
  693.5 112.7 %all-reduce.35.cloned.1.call-start = ((), (), s32[]{:S(2)}) async-start(), calls=%async_computation.10 | async-start | bytes 1048576 | tf_op jit(solution)/shard_map/psum | solution.py:46
  733.8 173.8 %all-reduce.37.cloned.1.call-start = ((), (), s32[]{:S(2)}) async-start(), calls=%async_computation.11 | async-start | bytes 2097152 | tf_op jit(solution)/shard_map/psum | solution.py:46
  823.2 128.9 %copy-start.6 = (f32[1024,64]{0,1:T(8,128)S(1)}, f32[1024,64]{0,1:T(8,128)}, u32[]{:S(2)}) copy-start(f32[1024,64]{0,1:T(8,128)} %all-reduce.33.cloned.1.call-done) | copy-start | bytes 786436
  830.6 203.4 %copy-start.4 = (f32[2048,64]{0,1:T(8,128)S(1)}, f32[2048,64]{0,1:T(8,128)}, u32[]{:S(2)}) copy-start(f32[2048,64]{0,1:T(8,128)} %all-reduce.31.cloned.1.call-done) | copy-start | bytes 1572868
  830.6 121.5 %all-reduce.39.cloned.1.call-start = ((), (), s32[]{:S(2)}) async-start(), calls=%async_computation.12 | async-start | bytes 524288 | tf_op jit(solution)/shard_map/psum | solution.py:42
  920.4 113.6 %all-reduce.41.cloned.1.call-start = ((), (), s32[]{:S(2)}) async-start(), calls=%async_computation.13 | async-start | bytes 1048576 | tf_op jit(solution)/shard_map/psum | solution.py:46
  961.5 123.0 %all-reduce.43.cloned.1.call-start = ((), (), s32[]{:S(2)}) async-start(), calls=%async_computation.14 | async-start | bytes 524288 | tf_op jit(solution)/shard_map/psum | solution.py:42
  1041.6 52.3 %copy-start.5 = (f32[2048,64]{0,1:T(8,128)}, f32[2048,64]{0,1:T(8,128)S(1)}, u32[]{:S(2)}) copy-start(f32[2048,64]{0,1:T(8,128)S(1)} %multiply_add_fusion) | copy-start | bytes 1572868
  1052.9 113.6 %all-reduce.45.cloned.1.call-start = ((), (), s32[]{:S(2)}) async-start(), calls=%async_computation.15 | async-start | bytes 1048576 | tf_op jit(solution)/shard_map/psum | solution.py:46
Sparse Core Ops, SparseCore 0:
  12.7 76.0 all-gather.3
  109.9 76.3 all-reduce.16
  199.2 31.5 all-reduce.18
  240.3 72.3 all-reduce.20
  325.1 31.2 all-reduce.22
  366.0 72.3 all-reduce.24
  462.8 76.6 all-reduce.26
  552.3 31.5 all-reduce.28
  593.5 72.2 all-reduce.30
  693.6 30.6 all-reduce.32
  733.9 72.2 all-reduce.34
  830.7 76.8 all-reduce.36
  920.5 31.5 all-reduce.38
  961.6 72.3 all-reduce.40
  1053.0 31.4 all-reduce.42
  1094.0 72.3 all-reduce.44
